TPU v7x, 32 devices: a whole 2x2x4 slice. The times are simulated.
32 devices in a mesh: groups: 2 (over x), seq: 16 (over z, y, core).
Axes of the slice: x: 2, y: 2, z: 4, core: 2. Of those that a mesh axis runs over, the one named last changes fastest.
Arguments:
- features: bfloat16 [16384, 768], P(('groups', 'seq')), parts along dimension 0, may hold values from -54 to 54
- bases: int32 [16384], P(('groups', 'seq')), parts along dimension 0, may hold values from 0 to 3
- base_table: bfloat16 [4, 768], replicated, may hold values from -3 to 3
- norm_gain: bfloat16 [768], replicated, may hold values from 0.25 to 1.75
- conv_weight: bfloat16 [5, 768, 768], replicated, may hold values from -0.09375 to 0.09375
- donor_proj: bfloat16 [768, 768], replicated, may hold values from -0.21875 to 0.21875
- acceptor_proj: bfloat16 [768, 768], replicated, may hold values from -0.21875 to 0.21875
- track_weight: bfloat16 [256, 768], replicated, may hold values from -0.375 to 0.375
- donor_offset: int32 [8192], P(('groups', 'seq')), parts along dimension 0, may hold values from 0 to 511
- acceptor_shard: int32 [8192, 1], P(('groups', 'seq')), parts along dimension 0, may hold values from 0 to 15; in each aligned block of 256 rows (0 to 255, 256 to 511, ...) at most 32 rows name the same one
- acceptor_offset: int32 [8192], P(('groups', 'seq')), parts along dimension 0, may hold values from 0 to 511
- junction_cotangent: bfloat16 [8192, 256], P(('groups', 'seq')), parts along dimension 0, may hold values from -6 to 6
Outputs:
- block_out: bfloat16 [16384, 768], P(('groups', 'seq')), parts along dimension 0
- head_grad: float32 [16384, 768], P(('groups', 'seq')), parts along dimension 0
There are 2 independent parts, one for each index of `groups`. A program takes and returns all parts, laid end to end along the dimension named above; an argument that names none is the same for every part. Nothing has to cross between parts.
Inputs may be any that keep to these rules, and one draw needn't show every extreme that they name: `acceptor_shard`: in each device's list (aligned blocks of 256 junctions), at most 32 junctions name any one shard.
All inputs are finite; a program needn't handle non-finite values.
Results may differ from a plain program's by a relative error of at most 0.0059.
Values may be sent and summed in bfloat16 or wider, within the bound.
A program may use at most 64 MiB of HBM per device.

v0:
```python
import jax
import jax.numpy as jnp
from jax import lax
from jax.sharding import PartitionSpec as P


def padded_2(block, sides, width):
    for axis, dim in sides:
        count = lax.axis_size(axis)
        forward = [(i, i + 1) for i in range(count - 1)]
        backward = [(target, source) for source, target in forward]
        low = lax.ppermute(
            lax.slice_in_dim(block, block.shape[dim] - width, None, axis=dim), axis, forward
        )
        high = lax.ppermute(lax.slice_in_dim(block, 0, width, axis=dim), axis, backward)
        block = jnp.concatenate([low, block, high], axis=dim)
    return block


def on_device(
    features,
    bases,
    base_table,
    norm_gain,
    conv_weight,
    donor_proj,
    acceptor_proj,
    track_weight,
    donor_offset,
    acceptor_shard,
    acceptor_offset,
    junction_cotangent,
):
    row_count = features.shape[0]
    channel_count = features.shape[1]
    pair_count = donor_proj.shape[1]
    track_count = track_weight.shape[0]
    base_rows = base_table.astype(jnp.float32)
    letters = bases[:, None]
    base_added = jnp.zeros(features.shape, jnp.float32)
    for letter in range(4):
        base_added = base_added + jnp.where(letters == letter, base_rows[letter][None, :], 0.0)
    embedded = features.astype(jnp.float32) + base_added
    square_mean = jnp.mean(embedded * embedded, axis=1, keepdims=True)
    normed = (
        embedded * lax.rsqrt(square_mean + 1e-06) * norm_gain.astype(jnp.float32)[None, :]
    ).astype(jnp.bfloat16)
    padded = padded_2(normed, (("seq", 0),), 2)
    conv_out = jnp.zeros(embedded.shape, jnp.float32)
    for position in range(conv_weight.shape[0]):
        conv_out = conv_out + jnp.dot(
            padded[position : position + row_count],
            conv_weight[position],
            preferred_element_type=jnp.float32,
        )
    block_out = (embedded + jax.nn.gelu(conv_out, approximate=False)).astype(jnp.bfloat16)
    donor_emb = jnp.dot(block_out, donor_proj, preferred_element_type=jnp.float32).astype(
        jnp.bfloat16
    )
    acceptor_emb = jnp.dot(block_out, acceptor_proj, preferred_element_type=jnp.float32).astype(
        jnp.bfloat16
    )
    shards = lax.axis_size("seq")
    junction_count = donor_offset.shape[0]
    capacity = 2 * junction_count // shards
    owner_shard = acceptor_shard[:, 0]
    onehot = (owner_shard[:, None] == jnp.arange(shards, dtype=jnp.int32)[None, :]).astype(
        jnp.int32
    )
    before = jnp.cumsum(onehot, axis=0) - onehot
    rank_in = jnp.sum(before * onehot, axis=1)
    slot_index = owner_shard * capacity + rank_in

    def bucket(values):
        buffer = (
            jnp.zeros((shards * capacity,) + values.shape[1:], values.dtype)
            .at[slot_index]
            .set(values)
        )
        return buffer.reshape((shards, capacity) + values.shape[1:])

    head_grad = jnp.zeros((row_count, channel_count), jnp.float32)
    sent_rows = lax.all_to_all(
        bucket(donor_emb[donor_offset]), "seq", split_axis=0, concat_axis=0, tiled=True
    )
    cotangents = lax.all_to_all(
        bucket(junction_cotangent), "seq", split_axis=0, concat_axis=0, tiled=True
    )
    offsets = lax.all_to_all(
        bucket(acceptor_offset), "seq", split_axis=0, concat_axis=0, tiled=True
    )
    slot_total = sent_rows.shape[0] * sent_rows.shape[1]
    coefficient = jnp.dot(
        cotangents.reshape(slot_total, track_count),
        track_weight,
        preferred_element_type=jnp.float32,
    )
    acceptor_grad = (
        coefficient * sent_rows.reshape(slot_total, pair_count).astype(jnp.float32)
    ).astype(jnp.bfloat16)
    local_rows = acceptor_emb[offsets.reshape(slot_total)]
    donor_grad = (coefficient * local_rows.astype(jnp.float32)).astype(jnp.bfloat16)
    contrib = jnp.dot(acceptor_grad, acceptor_proj.T, preferred_element_type=jnp.float32)
    contrib = contrib.reshape(sent_rows.shape[0], sent_rows.shape[1], channel_count)
    returned_rows = lax.all_to_all(
        donor_grad.reshape(sent_rows.shape), "seq", split_axis=0, concat_axis=0, tiled=True
    )
    contrib, got_offsets, returned_rows = (contrib, offsets, returned_rows)
    head_grad = head_grad.at[got_offsets.reshape(-1)].add(contrib.reshape(-1, channel_count))
    donor_grad = returned_rows.reshape(shards * capacity, pair_count)[slot_index]
    head_grad = head_grad.at[donor_offset].add(
        jnp.dot(donor_grad, donor_proj.T, preferred_element_type=jnp.float32)
    )
    return (block_out, head_grad)


def solution(mesh):
    in_specs = (
        P(("groups", "seq"), None),
        P(("groups", "seq")),
        P(),
        P(),
        P(),
        P(),
        P(),
        P(),
        P(("groups", "seq")),
        P(("groups", "seq"), None),
        P(("groups", "seq")),
        P(("groups", "seq"), None),
    )
    out_specs = (P(("groups", "seq"), None), P(("groups", "seq"), None))
    return jax.shard_map(
        on_device, mesh=mesh, in_specs=in_specs, out_specs=out_specs, check_vma=False
    )
```

profile of v0, /device:TPU:0, one launch (start us, length us, event | category | flops | bytes accessed | tf_op | source)
XLA Modules:
  0.0 115.2 jit_solution(2856237365425613928)
XLA Ops:
  0.7 0.8 convert_element_type.44
  1.5 0.7 broadcast_compare_fusion.3
  2.2 2.0 %multiply_reduce_fusion = f32[512]{0:T(512)S(1)} fusion(bf16[512,768]{1,0:T(8,128)(2,1)} %param.12, f32[768]{0:T(1024)S(1)} %get-tuple-element.3, f32[768]{0:T(1024)S(1)} %get-tuple-element.4, f32[768]{0:T(1024)S(1)} %get-tuple-element.5, f32[768]{0:T(1024)S(1)} %get-tuple-element.2, pred[512]{0:T(512)(128)(4,1)S(1)} %get-tuple-element.10, ...), kind=kLoop, calls=%fused_computation.31 | loop fusion | flops 4324864 | bytes 802816 | tf_op jit(solution)/shard_map/reduce_sum | solution.py:44
  4.8 1.9 %multiply_convert_fusion.1 = bf16[512,768]{1,0:T(8,128)(2,1)S(1)} fusion(bf16[512,768]{1,0:T(8,128)(2,1)} %param.12, f32[768]{0:T(1024)S(1)} %convert_element_type.45, f32[512]{0:T(512)S(1)} %add_rsqrt_fusion, f32[768]{0:T(1024)S(1)} %get-tuple-element.3, f32[768]{0:T(1024)S(1)} %get-tuple-element.4, f32[768]{0:T(1024)S(1)} %get-tuple-element.5, ...), kind=kLoop, calls=%fused_computation.30 | loop fusion | flops 4718592 | bytes 1592320 | tf_op jit(solution)/shard_map/convert_element_type | solution.py:47
  6.7 2.4 %collective-permute-start = (bf16[2,768]{1,0:T(2,128)(2,1)S(1)}, bf16[2,768]{1,0:T(2,128)(2,1)S(1)}, u32[]{:S(2)}, u32[]{:S(2)}) collective-permute-start(bf16[2,768]{1,0:T(2,128)(2,1)S(1)} %get-tuple-element.6), channel_id=1, source_target_pairs={{0,1},{1,2},{2,3},{3,4},{4,5},{5,6},{6,7},{7,8},{8,9},{9,10},{10,1... | collective-permute-start | bytes 9224 | tf_op jit(solution)/shard_map/ppermute | solution.py:12
  9.1 1.3 %collective-permute-start.1 = (bf16[2,768]{1,0:T(2,128)(2,1)S(1)}, bf16[2,768]{1,0:T(2,128)(2,1)S(1)}, u32[]{:S(2)}, u32[]{:S(2)}) collective-permute-start(bf16[2,768]{1,0:T(2,128)(2,1)S(1)} %get-tuple-element.7), channel_id=1, source_target_pairs={{1,0},{2,1},{3,2},{4,3},{5,4},{6,5},{7,6},{8,7},{9,8},{10,9},{11,1... | collective-permute-start | bytes 9224 | tf_op jit(solution)/shard_map/ppermute | solution.py:15
  11.3 1.6 %scatter_custom_fusion = s32[512]{0:T(512)S(1)} fusion(s32[256]{0:T(256)S(1)} %bitcast.66, s32[256]{0:T(256)} %param.22, s32[]{:T(128)} %constant.39.clone.1), kind=kCustom, calls=%fused_computation.93 | custom fusion | bytes 2560 | tf_op jit(solution)/shard_map/scatter | solution.py:78
  13.6 9.3 %all-to-all-start = ((s32[16,1,32]{2,1,0:T(1,128)}), s32[16,1,32]{2,1,0:T(1,128)S(1)}, u32[]{:S(2)}, u32[]{:S(2)}) async-start(s32[16,1,32]{2,1,0:T(1,128)} %all_to_all.15), calls=%async_computation | async-start | bytes 16384 | tf_op jit(solution)/shard_map/all_to_all | solution.py:89
  22.9 3.2 %fusion.18 = f32[512,768]{1,0:T(8,128)} fusion(bf16[512,768]{1,0:T(8,128)(2,1)S(1)} %multiply_convert_fusion.1, bf16[5,768,768]{2,1,0:T(8,128)(2,1)} %param.16), kind=kOutput, calls=%fused_computation.41 | convolution fusion | flops 603979776 | bytes 3538944 | tf_op jit(solution)/shard_map/dot_general | solution.py:51
  26.1 2.5 %scatter_custom_fusion.1 = bf16[512,256]{1,0:T(8,128)(2,1)} fusion(s32[256]{0:T(256)S(1)} %bitcast.67, bf16[256,256]{1,0:T(8,128)(2,1)} %param.23, bf16[]{:T(256)} %constant.35.clone.1), kind=kCustom, calls=%fused_computation.68 | custom fusion | bytes 262656 | tf_op jit(solution)/shard_map/scatter | solution.py:78
  28.7 3.2 %fusion.20 = f32[512,768]{1,0:T(8,128)} fusion(bf16[5,768,768]{2,1,0:T(8,128)(2,1)} %param.16, bf16[512,768]{1,0:T(8,128)(2,1)S(1)} %multiply_convert_fusion.1, bf16[2,768]{1,0:T(2,128)(2,1)S(1)} %collective-permute-done), kind=kOutput, calls=%fused_computation.43 | convolution fusion | flops 605552640 | bytes 3542016 | tf_op jit(solution)/shard_map/dot_general | solution.py:51
  31.9 3.2 %fusion.22 = f32[512,768]{1,0:T(8,128)} fusion(bf16[5,768,768]{2,1,0:T(8,128)(2,1)} %param.16, bf16[2,768]{1,0:T(2,128)(2,1)S(1)} %collective-permute-done, bf16[512,768]{1,0:T(8,128)(2,1)S(1)} %multiply_convert_fusion.1), kind=kOutput, calls=%fused_computation.45 | convolution fusion | flops 605552640 | bytes 3542016 | tf_op jit(solution)/shard_map/dot_general | solution.py:51
  35.1 3.3 %fusion.16 = f32[512,768]{1,0:T(8,128)} fusion(bf16[5,768,768]{2,1,0:T(8,128)(2,1)} %param.16, bf16[512,768]{1,0:T(8,128)(2,1)S(1)} %multiply_convert_fusion.1, bf16[2,768]{1,0:T(2,128)(2,1)S(1)} %collective-permute-done.1), kind=kOutput, calls=%fused_computation.39 | convolution fusion | flops 605552640 | bytes 3542016 | tf_op jit(solution)/shard_map/dot_general | solution.py:51
  38.3 6.0 %all-to-all-start.1 = ((bf16[16,32,256]{2,1,0:T(8,128)(2,1)}), bf16[16,32,256]{2,1,0:T(8,128)(2,1)S(1)}, u32[]{:S(2)}, u32[]{:S(2)}) async-start(bf16[16,32,256]{2,1,0:T(8,128)(2,1)} %bitcast.11), calls=%async_computation.1 | async-start | bytes 524288 | tf_op jit(solution)/shard_map/all_to_all | solution.py:86
  44.4 7.4 %fusion.3 = bf16[512,768]{1,0:T(8,128)(2,1)S(1)} fusion(f32[512,768]{1,0:T(8,128)} %fusion.16, f32[512,768]{1,0:T(8,128)} %fusion.18, f32[512,768]{1,0:T(8,128)} %fusion.22, f32[512,768]{1,0:T(8,128)} %fusion.20, bf16[5,768,768]{2,1,0:T(8,128)(2,1)} %param.16, bf16[512,768]{1,0:T(8,128)(2,1)S(1)} %copy-done.3, ...), kind=kOutput, calls=%fused_computation.12 | convolution fusion | flops 636616704 | bytes 9847808 | tf_op jit(solution)/shard_map/dot_general | solution.py:51
  51.8 0.9 copy-done.8
  52.7 0.8 convolution_convert_fusion.1
  53.5 4.1 %scatter_custom_fusion.2 = bf16[512,768]{1,0:T(8,128)(2,1)} fusion(s32[256]{0:T(256)S(1)} %bitcast.68, bf16[512,768]{1,0:T(8,128)(2,1)S(1)} %convolution_convert_fusion.1, s32[1024]{0:T(1024)S(1)} %pad_clamp_fusion.2, bf16[]{:T(256)} %constant.35.clone.1), kind=kCustom, calls=%fused_computation.65 | custom fusion | bytes 786434 | tf_op jit(solution)/shard_map/scatter | solution.py:78
  57.5 6.0 %all-to-all-start.2 = ((bf16[16,32,768]{2,1,0:T(8,128)(2,1)}), bf16[16,32,768]{2,1,0:T(8,128)(2,1)S(1)}, u32[]{:S(2)}, u32[]{:S(2)}) async-start(bf16[16,32,768]{2,1,0:T(8,128)(2,1)} %bitcast.13), calls=%async_computation.2 | async-start | bytes 1572864 | tf_op jit(solution)/shard_map/all_to_all | solution.py:83
  63.6 1.9 %convolution_convert_fusion = bf16[512,768]{1,0:T(8,128)(2,1)S(1)} fusion(bf16[512,768]{1,0:T(8,128)(2,1)} %copy-done.8, bf16[768,768]{1,0:T(8,128)(2,1)S(1)} %copy-done), kind=kOutput, calls=%fused_computation.35 | convolution fusion | flops 604372992 | bytes 2752512 | tf_op jit(solution)/shard_map/dot_general | solution.py:60
  66.8 2.7 %gather_fusion = bf16[512,768]{1,0:T(8,128)(2,1)} fusion(bf16[512,768]{1,0:T(8,128)(2,1)S(1)} %convolution_convert_fusion, s32[1024]{0:T(1024)S(1)} %pad_clamp_fusion.1), kind=kCustom, calls=%fused_computation.1 | custom fusion | bytes 1574912 | tf_op jit(solution)/shard_map/gather | solution.py:101
  69.5 2.6 %multiply_convert_fusion = (bf16[512,768]{1,0:T(8,128)(2,1)}, f32[512,768]{1,0:T(8,128)S(1)}) fusion(bf16[512,768]{1,0:T(8,128)(2,1)} %gather_fusion, bf16[512,256]{1,0:T(8,128)(2,1)} %bitcast.61, bf16[256,768]{1,0:T(8,128)(2,1)} %param.19), kind=kOutput, calls=%fused_computation.15 | convolution fusion | flops 202506240 | bytes 3801088 | tf_op jit(solution)/shard_map/dot_general | solution.py:93
  72.1 10.2 %all-to-all-done.2 = bf16[16,32,768]{2,1,0:T(8,128)(2,1)S(1)} async-done(((bf16[16,32,768]{2,1,0:T(8,128)(2,1)}), bf16[16,32,768]{2,1,0:T(8,128)(2,1)S(1)}, u32[]{:S(2)}, u32[]{:S(2)}) %all-to-all-start.2) | async-done | bytes 786464 | tf_op jit(solution)/shard_map/all_to_all | solution.py:83
  82.3 0.9 copy-done.2
  83.2 5.5 %all-to-all-start.3 = ((bf16[16,32,768]{2,1,0:T(8,128)(2,1)}), bf16[16,32,768]{2,1,0:T(8,128)(2,1)S(1)}, u32[]{:S(2)}, u32[]{:S(2)}) async-start(bf16[16,32,768]{2,1,0:T(8,128)(2,1)} %bitcast.60), calls=%async_computation.3 | async-start | bytes 1572864 | tf_op jit(solution)/shard_map/all_to_all | solution.py:105
  88.7 3.1 %fusion.33 = f32[512,768]{1,0:T(8,128)} fusion(bf16[768,768]{1,0:T(8,128)(2,1)S(1)} %copy-done, f32[512,768]{1,0:T(8,128)S(1)} %get-tuple-element.13, bf16[512,768]{1,0:T(8,128)(2,1)} %bitcast.59), kind=kOutput, calls=%fused_computation.58 | convolution fusion | flops 605159424 | bytes 5111808 | tf_op jit(solution)/shard_map/dot_general | solution.py:103
  91.8 5.1 %scatter_custom_fusion.3 = f32[512,768]{1,0:T(8,128)S(1)} fusion(s32[512]{0:T(512)S(1)} %bitcast.65, f32[512,768]{1,0:T(8,128)} %fusion.33, f32[]{:T(128)} %constant.40.clone.1), kind=kCustom, calls=%fused_computation.63 | custom fusion | flops 393216 | bytes 1573376 | tf_op jit(solution)/shard_map/scatter-add | solution.py:109
  96.9 10.5 %all-to-all-done.3 = bf16[16,32,768]{2,1,0:T(8,128)(2,1)S(1)} async-done(((bf16[16,32,768]{2,1,0:T(8,128)(2,1)}), bf16[16,32,768]{2,1,0:T(8,128)(2,1)S(1)}, u32[]{:S(2)}, u32[]{:S(2)}) %all-to-all-start.3) | async-done | bytes 786464 | tf_op jit(solution)/shard_map/all_to_all | solution.py:105
  107.4 1.9 %gather_fusion.1 = bf16[256,768]{1,0:T(8,128)(2,1)} fusion(bf16[512,768]{1,0:T(8,128)(2,1)S(1)} %bitcast.58, s32[1024]{0:T(1024)S(1)} %pad_clamp_fusion), kind=kCustom, calls=%fused_computation.2 | custom fusion | bytes 787456 | tf_op jit(solution)/shard_map/gather | solution.py:110
  109.3 1.9 %fusion.55 = f32[256,768]{1,0:T(8,128)S(1)} fusion(bf16[256,768]{1,0:T(8,128)(2,1)} %gather_fusion.1, bf16[768,768]{1,0:T(8,128)(2,1)} %param.17), kind=kOutput, calls=%fused_computation.101 | convolution fusion | flops 301989888 | bytes 2359296 | tf_op jit(solution)/shard_map/dot_general | solution.py:112
  111.2 2.8 %scatter_fusion = f32[512,768]{1,0:T(8,128)S(1)} fusion(f32[512,768]{1,0:T(8,128)S(1)} %scatter_custom_fusion.3, s32[256]{0:T(256)S(1)} %compare_select_fusion.2, f32[256,768]{1,0:T(8,128)S(1)} %fusion.55), kind=kCustom, calls=%fused_computation.7 | custom fusion | flops 196608 | bytes 2360320 | tf_op jit(solution)/shard_map/scatter-add | solution.py:111
  114.0 1.1 copy-done.1
  (39 shorter events, 3.7 us)
Async XLA Ops:
  0.6 62.9 %copy-start = (bf16[768,768]{1,0:T(8,128)(2,1)S(1)}, bf16[768,768]{1,0:T(8,128)(2,1)}, u32[]{:S(2)}) copy-start(bf16[768,768]{1,0:T(8,128)(2,1)} %param.18) | copy-start | bytes 3538948
  0.6 9.8 %copy-start.6 = (s32[256,1]{0,1:T(1,128)S(1)}, s32[256,1]{0,1:T(1,128)}, u32[]{:S(2)}) copy-start(s32[256,1]{0,1:T(1,128)} %param.21) | copy-start | bytes 3076
  6.7 21.9 %collective-permute-start = (bf16[2,768]{1,0:T(2,128)(2,1)S(1)}, bf16[2,768]{1,0:T(2,128)(2,1)S(1)}, u32[]{:S(2)}, u32[]{:S(2)}) collective-permute-start(bf16[2,768]{1,0:T(2,128)(2,1)S(1)} %get-tuple-element.6), channel_id=1, source_target_pairs={{0,1},{1,2},{2,3},{3,4},{4,5},{5,6},{6,7},{7,8},{8,9},{9,10},{10,1... | collective-permute-start | bytes 9224 | tf_op jit(solution)/shard_map/ppermute | solution.py:12
  9.1 26.0 %collective-permute-start.1 = (bf16[2,768]{1,0:T(2,128)(2,1)S(1)}, bf16[2,768]{1,0:T(2,128)(2,1)S(1)}, u32[]{:S(2)}, u32[]{:S(2)}) collective-permute-start(bf16[2,768]{1,0:T(2,128)(2,1)S(1)} %get-tuple-element.7), channel_id=1, source_target_pairs={{1,0},{2,1},{3,2},{4,3},{5,4},{6,5},{7,6},{8,7},{9,8},{10,9},{11,1... | collective-permute-start | bytes 9224 | tf_op jit(solution)/shard_map/ppermute | solution.py:15
  13.6 24.8 %all-to-all-start = ((s32[16,1,32]{2,1,0:T(1,128)}), s32[16,1,32]{2,1,0:T(1,128)S(1)}, u32[]{:S(2)}, u32[]{:S(2)}) async-start(s32[16,1,32]{2,1,0:T(1,128)} %all_to_all.15), calls=%async_computation | async-start | bytes 16384 | tf_op jit(solution)/shard_map/all_to_all | solution.py:89
  22.9 3.2 %copy-start.7 = (s32[256]{0:T(256)S(1)}, s32[256]{0:T(256)}, u32[]{:S(2)}) copy-start(s32[256]{0:T(256)} %param.20) | copy-start | bytes 3076
  35.1 9.3 %copy-start.3 = (bf16[512,768]{1,0:T(8,128)(2,1)S(1)}, bf16[512,768]{1,0:T(8,128)(2,1)}, u32[]{:S(2)}) copy-start(bf16[512,768]{1,0:T(8,128)(2,1)} %param.12) | copy-start | bytes 2359300
  38.3 19.2 %all-to-all-start.1 = ((bf16[16,32,256]{2,1,0:T(8,128)(2,1)}), bf16[16,32,256]{2,1,0:T(8,128)(2,1)S(1)}, u32[]{:S(2)}, u32[]{:S(2)}) async-start(bf16[16,32,256]{2,1,0:T(8,128)(2,1)} %bitcast.11), calls=%async_computation.1 | async-start | bytes 524288 | tf_op jit(solution)/shard_map/all_to_all | solution.py:86
  44.4 8.3 %copy-start.4 = (bf16[768,768]{1,0:T(8,128)(2,1)S(1)}, bf16[768,768]{1,0:T(8,128)(2,1)}, u32[]{:S(2)}) copy-start(bf16[768,768]{1,0:T(8,128)(2,1)} %param.17) | copy-start | bytes 3538948
  51.8 0.9 copy-start.8
  57.5 8.0 %copy-start.5 = (bf16[16,32,256]{2,1,0:T(8,128)(2,1)}, bf16[16,32,256]{2,1,0:T(8,128)(2,1)S(1)}, u32[]{:S(2)}) copy-start(bf16[16,32,256]{2,1,0:T(8,128)(2,1)S(1)} %all-to-all-done.1) | copy-start | bytes 786436
  57.5 24.7 %all-to-all-start.2 = ((bf16[16,32,768]{2,1,0:T(8,128)(2,1)}), bf16[16,32,768]{2,1,0:T(8,128)(2,1)S(1)}, u32[]{:S(2)}, u32[]{:S(2)}) async-start(bf16[16,32,768]{2,1,0:T(8,128)(2,1)} %bitcast.13), calls=%async_computation.2 | async-start | bytes 1572864 | tf_op jit(solution)/shard_map/all_to_all | solution.py:83
  82.3 0.9 copy-start.2
  83.2 24.2 %all-to-all-start.3 = ((bf16[16,32,768]{2,1,0:T(8,128)(2,1)}), bf16[16,32,768]{2,1,0:T(8,128)(2,1)S(1)}, u32[]{:S(2)}, u32[]{:S(2)}) async-start(bf16[16,32,768]{2,1,0:T(8,128)(2,1)} %bitcast.60), calls=%async_computation.3 | async-start | bytes 1572864 | tf_op jit(solution)/shard_map/all_to_all | solution.py:105
  114.0 1.1 copy-start.1
where the time goes:
time: 116 us; the launch traced here: 115 us
  matrix products  30.6 us (26%)
  starting transfers between devices  30.4 us (26%)
  waiting for transfers between devices  20.7 us (18%)
  local copies, waits for them, and re-layouts  17.2 us (15%)
  other arithmetic  15.4 us (13%)
    dot_general x5, matrix products, on_device(): jnp.dot(padded[position:position + row_count], conv_weight[position], pre...  20.3 us
    all_to_all x1, waiting for transfers between devices, on_device(): lax.all_to_all(donor_grad.reshape(sent_rows.shape), 'seq', split_axis=0,...  10.5 us
    all_to_all x1, waiting for transfers between devices, on_device(): lax.all_to_all(bucket(donor_emb[donor_offset]), 'seq', split_axis=0, conc...  10.2 us
    all_to_all x1, starting transfers between devices, on_device(): lax.all_to_all(bucket(acceptor_offset), 'seq', split_axis=0, concat_axis=...  9.3 us
    scatter x3, local copies, waits for them, and re-layouts, bucket(): buffer = jnp.zeros((shards * capacity,) + values.shape[1:], values.dtype)...  8.14 us
    all_to_all x1, starting transfers between devices, on_device(): lax.all_to_all(bucket(donor_emb[donor_offset]), 'seq', split_axis=0, conc...  6.02 us
    all_to_all x1, starting transfers between devices, on_device(): lax.all_to_all(bucket(junction_cotangent), 'seq', split_axis=0, concat_ax...  6.01 us
    all_to_all x1, starting transfers between devices, on_device(): lax.all_to_all(donor_grad.reshape(sent_rows.shape), 'seq', split_axis=0,...  5.47 us
  transfers between devices with their start and end apart: 6, of which 2 were waited for; matrix products, arithmetic and copies ran while one was open for 41% of the time, Pallas kernels for 0%

commit v1 on v0

v1 whole, which is shorter than its diff:
```python
import functools

import jax
import jax.numpy as jnp
from jax import lax
from jax.experimental import pallas as pl
from jax.experimental.pallas import tpu as pltpu
from jax.sharding import PartitionSpec as P

F32 = jnp.float32
BF16 = jnp.bfloat16
I32 = jnp.int32
EDGE = 8


def iota(shape, dim):
    return lax.broadcasted_iota(I32, shape, dim)


def to_column(row):
    size = row.shape[1]
    eye = iota((size, size), 0) == iota((size, size), 1)
    return jnp.sum(jnp.where(eye, row, 0), axis=1, keepdims=True)


def dot(a, b):
    return jnp.dot(a, b, preferred_element_type=F32)


def dot_t(a, b):
    return lax.dot_general(a, b, (((1,), (1,)), ((), ())), preferred_element_type=F32)


def kernel(
    n,
    cap,
    feat_ref,
    bases_ref,
    table_ref,
    gain_ref,
    conv_hbm,
    donor_hbm,
    acceptor_hbm,
    track_ref,
    doff_ref,
    owner_ref,
    aoff_ref,
    cot_ref,
    block_ref,
    head_ref,
    npad,
    emb,
    xcol,
    conv_w,
    donor_w,
    acceptor_w,
    demb,
    aemb,
    coef,
    send_a,
    recv_a,
    send_b,
    recv_b,
    offs_send,
    offs_recv,
    doff_col,
    doff_row,
    aoff_col,
    scat_a,
    scat_d,
    local_sem,
    halo_send,
    halo_recv,
    offs_ssem,
    offs_rsem,
    a_ssem,
    a_rsem,
    b_ssem,
    b_rsem,
):
    rows, channels = feat_ref.shape
    taps = conv_hbm.shape[0]
    juncs = cot_ref.shape[0]
    slots = n * cap
    tile = min(slots, 512)
    tiles = slots // tile
    me = lax.axis_index("seq")
    right = lax.rem(me + 1, n)
    left = lax.rem(me + n - 1, n)

    copies = [
        pltpu.make_async_copy(
            conv_hbm.at[t], conv_w.at[pl.ds(t * channels, channels)], local_sem.at[t]
        )
        for t in range(taps)
    ]
    copies.append(pltpu.make_async_copy(donor_hbm, donor_w, local_sem.at[taps]))
    copies.append(pltpu.make_async_copy(acceptor_hbm, acceptor_w, local_sem.at[taps + 1]))
    for copy in copies:
        copy.start()

    def partner(i):
        sign = 1 - 2 * lax.rem(i, 2)
        return lax.rem(me + n // 2 + sign * ((i + 1) // 2), n)

    barrier = pltpu.get_barrier_semaphore()

    @pl.loop(0, n - 1)
    def _(i):
        pl.semaphore_signal(barrier, inc=1, device_id={"seq": partner(i)})

    letters = to_column(bases_ref[...])
    table = table_ref[...].astype(F32)
    base = jnp.where(
        letters == 0,
        table[0:1],
        jnp.where(letters == 1, table[1:2], jnp.where(letters == 2, table[2:3], table[3:4])),
    )
    embedded = feat_ref[...].astype(F32) + base
    emb[...] = embedded
    scale = lax.rsqrt(jnp.mean(embedded * embedded, axis=1, keepdims=True) + 1e-06)
    normed = (embedded * scale * gain_ref[...].astype(F32)).astype(BF16)
    npad[pl.ds(EDGE, rows)] = normed.astype(F32)

    owner_row = owner_ref[...]
    owner_col = to_column(owner_row)
    earlier = iota((juncs, juncs), 0) < iota((juncs, juncs), 1)
    same = owner_col == owner_row
    rank_row = jnp.sum(jnp.where(same & earlier, 1, 0), axis=0, keepdims=True)
    rank_col = to_column(rank_row)
    slot_row = owner_row * cap + rank_row
    slot_col = owner_col * cap + rank_col
    aoff_by_rank = jnp.where(rank_col == iota((juncs, 128), 1), to_column(aoff_ref[...]), 0)

    @pl.loop(0, n)
    def _(p):
        row = jnp.sum(jnp.where(owner_col == p, aoff_by_rank, 0), axis=0, keepdims=True)
        offs_send[p] = jnp.broadcast_to(row, (8, 128))

    pl.semaphore_wait(barrier, n - 1)

    halo_right = pltpu.make_async_remote_copy(
        src_ref=npad.at[pl.ds(rows, EDGE)],
        dst_ref=npad.at[pl.ds(0, EDGE)],
        send_sem=halo_send.at[0],
        recv_sem=halo_recv.at[0],
        device_id={"seq": right},
    )
    halo_left = pltpu.make_async_remote_copy(
        src_ref=npad.at[pl.ds(EDGE, EDGE)],
        dst_ref=npad.at[pl.ds(EDGE + rows, EDGE)],
        send_sem=halo_send.at[1],
        recv_sem=halo_recv.at[1],
        device_id={"seq": left},
    )
    halo_right.start()
    halo_left.start()

    def offs_copy(p, slot):
        return pltpu.make_async_remote_copy(
            src_ref=offs_send.at[p],
            dst_ref=offs_recv.at[slot],
            send_sem=offs_ssem.at[p],
            recv_sem=offs_rsem.at[slot],
            device_id={"seq": p},
        )

    def rows_copy(src, dst, ssem, rsem, p, slot):
        return pltpu.make_async_remote_copy(
            src_ref=src.at[pl.ds(pl.multiple_of(p * cap, cap), cap)],
            dst_ref=dst.at[pl.ds(pl.multiple_of(slot * cap, cap), cap)],
            send_sem=ssem.at[p],
            recv_sem=rsem.at[slot],
            device_id={"seq": p},
        )

    @pl.loop(0, n - 1)
    def _(i):
        offs_copy(partner(i), me).start()

    donor_col = to_column(doff_ref[...])

    @pl.loop(0, tiles)
    def _(k):
        at = pl.ds(pl.multiple_of(k * tile, tile), tile)
        hit = (iota((tile, juncs), 0) + k * tile) == slot_row
        doff_col[at] = jnp.broadcast_to(
            jnp.sum(jnp.where(hit, doff_ref[...], 0), axis=1, keepdims=True), (tile, 128)
        )
        hit_t = slot_col == (iota((juncs, tile), 1) + k * tile)
        doff_row[k] = jnp.broadcast_to(
            jnp.sum(jnp.where(hit_t, donor_col, 0), axis=0, keepdims=True), (8, tile)
        )
        picked = dot(jnp.where(hit, 1.0, 0.0).astype(BF16), cot_ref[...]).astype(BF16)
        coef[at] = dot(picked, track_ref[...])

    halo_right.wait()
    halo_left.wait()

    @pl.when(me == 0)
    def _():
        npad[pl.ds(0, EDGE)] = jnp.zeros((EDGE, channels), F32)

    @pl.when(me == n - 1)
    def _():
        npad[pl.ds(EDGE + rows, EDGE)] = jnp.zeros((EDGE, channels), F32)

    for t in range(taps):
        xcol[:, pl.ds(t * channels, channels)] = npad[
            pl.ds(EDGE - taps // 2 + t, rows)
        ].astype(BF16)
    for copy in copies:
        copy.wait()

    @pl.loop(0, channels // 256)
    def _(c):
        cols = pl.ds(pl.multiple_of(c * 256, 256), 256)
        out = dot(xcol[...], conv_w[:, cols])
        act = 0.5 * out * (1.0 + lax.erf(out * (0.5**0.5)))
        block_ref[:, cols] = (emb[:, cols] + act).astype(BF16)

    demb[...] = dot(block_ref[...], donor_w[...]).astype(BF16)

    @pl.loop(0, tiles)
    def _(k):
        at = pl.ds(pl.multiple_of(k * tile, tile), tile)
        pick = jnp.where(doff_col[at][:, 0:1] == iota((tile, rows), 1), 1.0, 0.0).astype(BF16)
        send_a[at] = (coef[at] * dot(pick, demb[...])).astype(BF16)

    @pl.loop(0, n - 1)
    def _(i):
        rows_copy(send_a, recv_a, a_ssem, a_rsem, partner(i), me).start()

    aemb[...] = dot(block_ref[...], acceptor_w[...]).astype(BF16)

    @pl.loop(0, n - 1)
    def _(i):
        p = partner(i)
        offs_copy(p, me).wait_send()
        offs_copy(p, p).wait_recv()

    offs_recv[me] = offs_send[me]

    @pl.loop(0, n)
    def _(p):
        row = offs_recv[p][0:1]
        mask = iota((cap, 128), 0) == iota((cap, 128), 1)
        aoff_col[pl.ds(pl.multiple_of(p * cap, cap), cap)] = jnp.broadcast_to(
            jnp.sum(jnp.where(mask, row, 0), axis=1, keepdims=True), (cap, 128)
        )

    @pl.loop(0, tiles)
    def _(k):
        at = pl.ds(pl.multiple_of(k * tile, tile), tile)
        pick = jnp.where(aoff_col[at][:, 0:1] == iota((tile, rows), 1), 1.0, 0.0).astype(BF16)
        send_b[at] = dot(pick, aemb[...]).astype(BF16)

    @pl.loop(0, n - 1)
    def _(i):
        rows_copy(send_b, recv_b, b_ssem, b_rsem, partner(i), me).start()

    own = pl.ds(pl.multiple_of(me * cap, cap), cap)
    recv_a[own] = send_a[own]
    recv_b[own] = send_b[own]
    scat_a[...] = jnp.zeros_like(scat_a)
    scat_d[...] = jnp.zeros_like(scat_d)

    @pl.loop(0, n - 1)
    def _(i):
        p = partner(i)
        rows_copy(send_a, recv_a, a_ssem, a_rsem, p, p).wait_recv()

    @pl.loop(0, tiles)
    def _(k):
        at = pl.ds(pl.multiple_of(k * tile, tile), tile)
        eye = iota((tile, tile), 0) == iota((tile, tile), 1)
        where = jnp.sum(jnp.where(eye, aoff_col[at][:, 0:1], 0), axis=0, keepdims=True)
        put = jnp.where(iota((rows, tile), 0) == where, 1.0, 0.0).astype(BF16)
        scat_a[...] += dot(put, recv_a[at])

    head_ref[...] = dot_t(scat_a[...].astype(BF16), acceptor_w[...])

    @pl.loop(0, n - 1)
    def _(i):
        p = partner(i)
        rows_copy(send_b, recv_b, b_ssem, b_rsem, p, p).wait_recv()

    @pl.loop(0, tiles)
    def _(k):
        at = pl.ds(pl.multiple_of(k * tile, tile), tile)
        grad = (coef[at] * recv_b[at].astype(F32)).astype(BF16)
        put = jnp.where(iota((rows, tile), 0) == doff_row[k][0:1], 1.0, 0.0).astype(BF16)
        scat_d[...] += dot(put, grad)

    head_ref[...] += dot_t(scat_d[...].astype(BF16), donor_w[...])

    @pl.loop(0, n - 1)
    def _(i):
        p = partner(i)
        rows_copy(send_a, recv_a, a_ssem, a_rsem, p, me).wait_send()
        rows_copy(send_b, recv_b, b_ssem, b_rsem, p, me).wait_send()


def on_device(
    features,
    bases,
    base_table,
    norm_gain,
    conv_weight,
    donor_proj,
    acceptor_proj,
    track_weight,
    donor_offset,
    acceptor_shard,
    acceptor_offset,
    junction_cotangent,
):
    n = lax.axis_size("seq")
    rows, channels = features.shape
    taps = conv_weight.shape[0]
    pair = donor_proj.shape[1]
    juncs = donor_offset.shape[0]
    cap = max(2 * juncs // n, 16)
    slots = n * cap
    tile = min(slots, 512)
    vmem = pl.BlockSpec(memory_space=pltpu.VMEM)
    hbm = pl.BlockSpec(memory_space=pl.ANY)
    dma = pltpu.SemaphoreType.DMA
    return pl.pallas_call(
        functools.partial(kernel, n, cap),
        out_shape=(
            jax.ShapeDtypeStruct((rows, channels), BF16),
            jax.ShapeDtypeStruct((rows, channels), F32),
        ),
        in_specs=[vmem, vmem, vmem, vmem, hbm, hbm, hbm, vmem, vmem, vmem, vmem, vmem],
        out_specs=(vmem, vmem),
        scratch_shapes=[
            pltpu.VMEM((rows + 2 * EDGE, channels), F32),
            pltpu.VMEM((rows, channels), F32),
            pltpu.VMEM((rows, taps * channels), BF16),
            pltpu.VMEM((taps * channels, channels), BF16),
            pltpu.VMEM((channels, pair), BF16),
            pltpu.VMEM((channels, pair), BF16),
            pltpu.VMEM((rows, pair), BF16),
            pltpu.VMEM((rows, pair), BF16),
            pltpu.VMEM((slots, pair), F32),
            pltpu.VMEM((slots, pair), BF16),
            pltpu.VMEM((slots, pair), BF16),
            pltpu.VMEM((slots, pair), BF16),
            pltpu.VMEM((slots, pair), BF16),
            pltpu.VMEM((n, 8, 128), I32),
            pltpu.VMEM((n, 8, 128), I32),
            pltpu.VMEM((slots, 128), I32),
            pltpu.VMEM((slots // tile, 8, tile), I32),
            pltpu.VMEM((slots, 128), I32),
            pltpu.VMEM((rows, pair), F32),
            pltpu.VMEM((rows, pair), F32),
            dma((taps + 2,)),
            dma((2,)),
            dma((2,)),
            dma((n,)),
            dma((n,)),
            dma((n,)),
            dma((n,)),
            dma((n,)),
            dma((n,)),
        ],
        compiler_params=pltpu.CompilerParams(
            collective_id=0, has_side_effects=True, vmem_limit_bytes=58 * 1024 * 1024
        ),
        name="block_and_pairs",
    )(
        features,
        bases.reshape(1, rows),
        base_table,
        norm_gain.reshape(1, channels),
        conv_weight,
        donor_proj,
        acceptor_proj,
        track_weight,
        donor_offset.reshape(1, juncs),
        acceptor_shard.reshape(1, juncs),
        acceptor_offset.reshape(1, juncs),
        junction_cotangent,
    )


def solution(mesh):
    split = ("groups", "seq")
    in_specs = (
        P(split, None),
        P(split),
        P(),
        P(),
        P(),
        P(),
        P(),
        P(),
        P(split),
        P(split, None),
        P(split),
        P(split, None),
    )
    out_specs = (P(split, None), P(split, None))
    return jax.shard_map(
        on_device, mesh=mesh, in_specs=in_specs, out_specs=out_specs, check_vma=False
    )
```

time: 116 us -> 58.7 us (0.51)
  Pallas kernels: 0 us -> 53.2 us
  matrix products: 30.6 us -> 0 us
  starting transfers between devices: 30.4 us -> 0 us
  waiting for transfers between devices: 20.7 us -> 0 us
  other arithmetic: 15.4 us -> 0 us
  local copies, waits for them, and re-layouts: 17.2 us -> 4.59 us
    pallas_call x0 -> x1, Pallas kernels: none -> 53.2 us  [on_device(): pl.pallas_call(functools.partial(kernel, n, cap), out_shape=(jax.ShapeDty...]
    dot_general x10 -> x0, matrix products: 30.6 us -> none  [the longest x5 20.3 us: on_device(): jnp.dot(padded[position:position + row_count], conv_weight[position], pre...]
    all_to_all x4 -> x0, starting transfers between devices: 26.8 us -> none  [the longest x1 9.3 us: on_device(): lax.all_to_all(bucket(acceptor_offset), 'seq', split_axis=0, concat_axis=...]
    all_to_all x4 -> x0, waiting for transfers between devices: 20.7 us -> none  [the longest x1 10.5 us: on_device(): lax.all_to_all(donor_grad.reshape(sent_rows.shape), 'seq', split_axis=0,...]
    scatter x3 -> x0, local copies, waits for them, and re-layouts: 8.14 us -> none  [bucket(): buffer = jnp.zeros((shards * capacity,) + values.shape[1:], values.dtype)...]
    scatter-add x2 -> x0, other arithmetic: 7.93 us -> none  [the longest x1 5.11 us: on_device(): head_grad.at[got_offsets.reshape(-1)]]
    gather x2 -> x0, local copies, waits for them, and re-layouts: 4.64 us -> none  [the longest x1 2.71 us: on_device(): local_rows = acceptor_emb[offsets.reshape(slot_total)]]
    ppermute x2 -> x0, starting transfers between devices: 3.65 us -> none  [the longest x1 2.36 us: padded_2(): lax.ppermute(lax.slice_in_dim(block, block.shape[dim] - width, None, axis...]
  transfers between devices with their start and end apart: 6 -> 0, of which waited for: 2 -> 0; matrix products, arithmetic and copies ran while one was open for 41% -> 0% of each run, Pallas kernels for 0% -> 0%
where the time goes in v1:
time: 58.7 us; the launch traced here: 58.5 us
  Pallas kernels  53.2 us (91%)
  local copies, waits for them, and re-layouts  4.59 us (8%)
  between operations  0.65 us (1%)
    pallas_call x1, Pallas kernels, on_device(): pl.pallas_call(functools.partial(kernel, n, cap), out_shape=(jax.ShapeDty...  53.2 us
    unnamed x4, local copies, waits for them, and re-layouts  3.33 us
    reshape x1, local copies, waits for them, and re-layouts, on_device(): norm_gain.reshape(1, channels)  1.26 us

profile of v1, /device:TPU:0, one launch (start us, length us, event | category | flops | bytes accessed | tf_op | source)
XLA Modules:
  0.0 58.5 jit_solution(340005248568141518)
XLA Ops:
  0.6 1.3 %reshape.20.gain_ref = bf16[1,768]{1,0:T(2,128)(2,1)} reshape(bf16[768]{0:T(1024)(128)(2,1)} %param.15) | data formatting | bytes 3072 | tf_op jit(solution)/shard_map/reshape | solution.py:376
  1.9 53.2 %block_and_pairs.1 = (bf16[512,768]{1,0:T(8,128)(2,1)}, f32[512,768]{1,0:T(8,128)}) custom-call(bf16[512,768]{1,0:T(8,128)(2,1)} %feat_ref.1, s32[1,512]{1,0:T(1,128)} %bitcast.4, bf16[4,768]{1,0:T(4,128)(2,1)} %table_ref.1, bf16[1,768]{1,0:T(2,128)(2,1)} %reshape.20.gain_ref, bf16[5,768,768]{2,1,0:T(8,128)(2,1)} %conv_hbm.1, bf16[768,768]{1,0:T(8,128)(2,1)} %donor_hbm.1, ...), custom_call_target="tpu_custom_call" | custom-call | tf_op jit(solution)/shard_map/block_and_pairs/pallas_call | solution.py:329
  55.1 0.0 copy-start
  55.1 2.2 %copy.16 = bf16[512,768]{1,0:T(8,128)(2,1)} copy(bf16[512,768]{1,0:T(8,128)(2,1)} %get-tuple-element.4) | data formatting | bytes 1572864
  57.3 0.0 copy-done
  57.3 1.1 %copy.17 = f32[512,768]{1,0:T(8,128)} copy(f32[512,768]{1,0:T(8,128)S(1)} %copy-done) | data formatting | bytes 3145728
Async XLA Ops:
  55.1 2.2 %copy-start = (f32[512,768]{1,0:T(8,128)S(1)}, f32[512,768]{1,0:T(8,128)}, u32[]{:S(2)}) copy-start(f32[512,768]{1,0:T(8,128)} %get-tuple-element.5) | copy-start | bytes 4718596

commit v2 on v1

--- a/solution.py
+++ b/solution.py
@@ -11,6 +11,7 @@
 BF16 = jnp.bfloat16
 I32 = jnp.int32
 EDGE = 8
+WIDE = 256
 
 
 def iota(shape, dim):
@@ -46,8 +47,9 @@
     owner_ref,
     aoff_ref,
     cot_ref,
-    block_ref,
-    head_ref,
+    block_hbm,
+    head_hbm,
+    scat_hbm,
     npad,
     emb,
     xcol,
@@ -68,7 +70,13 @@
     aoff_col,
     scat_a,
     scat_d,
+    pick_b,
+    put_a,
+    block_ref,
+    head_ref,
+    scat_out,
     local_sem,
+    out_sem,
     halo_send,
     halo_recv,
     offs_ssem,
@@ -84,6 +92,7 @@
     slots = n * cap
     tile = min(slots, 512)
     tiles = slots // tile
+    chunks = donor_hbm.shape[1] // WIDE
     me = lax.axis_index("seq")
     right = lax.rem(me + 1, n)
     left = lax.rem(me + n - 1, n)
@@ -119,7 +128,7 @@
     embedded = feat_ref[...].astype(F32) + base
     emb[...] = embedded
     scale = lax.rsqrt(jnp.mean(embedded * embedded, axis=1, keepdims=True) + 1e-06)
-    normed = (embedded * scale * gain_ref[...].astype(F32)).astype(BF16)
+    normed = (embedded * scale * gain_ref[...].astype(F32)[None, :]).astype(BF16)
     npad[pl.ds(EDGE, rows)] = normed.astype(F32)
 
     owner_row = owner_ref[...]
@@ -165,34 +174,19 @@
             device_id={"seq": p},
         )
 
-    def rows_copy(src, dst, ssem, rsem, p, slot):
+    def rows_copy(src, dst, ssem, rsem, c, p, slot):
+        cols = pl.ds(c * WIDE, WIDE)
         return pltpu.make_async_remote_copy(
-            src_ref=src.at[pl.ds(pl.multiple_of(p * cap, cap), cap)],
-            dst_ref=dst.at[pl.ds(pl.multiple_of(slot * cap, cap), cap)],
-            send_sem=ssem.at[p],
-            recv_sem=rsem.at[slot],
+            src_ref=src.at[pl.ds(pl.multiple_of(p * cap, cap), cap), cols],
+            dst_ref=dst.at[pl.ds(pl.multiple_of(slot * cap, cap), cap), cols],
+            send_sem=ssem.at[c, p],
+            recv_sem=rsem.at[c, slot],
             device_id={"seq": p},
         )
 
     @pl.loop(0, n - 1)
     def _(i):
         offs_copy(partner(i), me).start()
-
-    donor_col = to_column(doff_ref[...])
-
-    @pl.loop(0, tiles)
-    def _(k):
-        at = pl.ds(pl.multiple_of(k * tile, tile), tile)
-        hit = (iota((tile, juncs), 0) + k * tile) == slot_row
-        doff_col[at] = jnp.broadcast_to(
-            jnp.sum(jnp.where(hit, doff_ref[...], 0), axis=1, keepdims=True), (tile, 128)
-        )
-        hit_t = slot_col == (iota((juncs, tile), 1) + k * tile)
-        doff_row[k] = jnp.broadcast_to(
-            jnp.sum(jnp.where(hit_t, donor_col, 0), axis=0, keepdims=True), (8, tile)
-        )
-        picked = dot(jnp.where(hit, 1.0, 0.0).astype(BF16), cot_ref[...]).astype(BF16)
-        coef[at] = dot(picked, track_ref[...])
 
     halo_right.wait()
     halo_left.wait()
@@ -209,29 +203,6 @@
         xcol[:, pl.ds(t * channels, channels)] = npad[
             pl.ds(EDGE - taps // 2 + t, rows)
         ].astype(BF16)
-    for copy in copies:
-        copy.wait()
-
-    @pl.loop(0, channels // 256)
-    def _(c):
-        cols = pl.ds(pl.multiple_of(c * 256, 256), 256)
-        out = dot(xcol[...], conv_w[:, cols])
-        act = 0.5 * out * (1.0 + lax.erf(out * (0.5**0.5)))
-        block_ref[:, cols] = (emb[:, cols] + act).astype(BF16)
-
-    demb[...] = dot(block_ref[...], donor_w[...]).astype(BF16)
-
-    @pl.loop(0, tiles)
-    def _(k):
-        at = pl.ds(pl.multiple_of(k * tile, tile), tile)
-        pick = jnp.where(doff_col[at][:, 0:1] == iota((tile, rows), 1), 1.0, 0.0).astype(BF16)
-        send_a[at] = (coef[at] * dot(pick, demb[...])).astype(BF16)
-
-    @pl.loop(0, n - 1)
-    def _(i):
-        rows_copy(send_a, recv_a, a_ssem, a_rsem, partner(i), me).start()
-
-    aemb[...] = dot(block_ref[...], acceptor_w[...]).astype(BF16)
 
     @pl.loop(0, n - 1)
     def _(i):
@@ -252,12 +223,62 @@
     @pl.loop(0, tiles)
     def _(k):
         at = pl.ds(pl.multiple_of(k * tile, tile), tile)
-        pick = jnp.where(aoff_col[at][:, 0:1] == iota((tile, rows), 1), 1.0, 0.0).astype(BF16)
-        send_b[at] = dot(pick, aemb[...]).astype(BF16)
-
-    @pl.loop(0, n - 1)
-    def _(i):
-        rows_copy(send_b, recv_b, b_ssem, b_rsem, partner(i), me).start()
+        hit = aoff_col[at][:, 0:1] == iota((tile, rows), 1)
+        pick_b[at] = jnp.where(hit, 1.0, 0.0).astype(BF16)
+
+    for copy in copies:
+        copy.wait()
+
+    for c in range(channels // WIDE):
+        cols = pl.ds(c * WIDE, WIDE)
+        out = dot(xcol[...], conv_w[:, cols])
+        act = 0.5 * out * (1.0 + lax.erf(out * (0.5**0.5)))
+        block_ref[:, cols] = (emb[:, cols] + act).astype(BF16)
+
+    for c in range(chunks):
+        cols = pl.ds(c * WIDE, WIDE)
+        aemb[...] = dot(block_ref[...], acceptor_w[:, cols]).astype(BF16)
+
+        @pl.loop(0, tiles)
+        def _(k):
+            at = pl.ds(pl.multiple_of(k * tile, tile), tile)
+            send_b[at, cols] = dot(pick_b[at], aemb[...]).astype(BF16)
+
+        @pl.loop(0, n - 1)
+        def _(i):
+            rows_copy(send_b, recv_b, b_ssem, b_rsem, c, partner(i), me).start()
+
+    block_out = pltpu.make_async_copy(block_ref, block_hbm, out_sem.at[0])
+    block_out.start()
+    donor_col = to_column(doff_ref[...])
+
+    @pl.loop(0, tiles)
+    def _(k):
+        at = pl.ds(pl.multiple_of(k * tile, tile), tile)
+        hit = (iota((tile, juncs), 0) + k * tile) == slot_row
+        doff_col[at] = jnp.broadcast_to(
+            jnp.sum(jnp.where(hit, doff_ref[...], 0), axis=1, keepdims=True), (tile, 128)
+        )
+        hit_t = slot_col == (iota((juncs, tile), 1) + k * tile)
+        doff_row[k] = jnp.broadcast_to(
+            jnp.sum(jnp.where(hit_t, donor_col, 0), axis=0, keepdims=True), (8, tile)
+        )
+        picked = dot(jnp.where(hit, 1.0, 0.0).astype(BF16), cot_ref[...]).astype(BF16)
+        coef[at] = dot(picked, track_ref[...])
+
+    demb[...] = dot(block_ref[...], donor_w[...]).astype(BF16)
+
+    @pl.loop(0, tiles)
+    def _(k):
+        at = pl.ds(pl.multiple_of(k * tile, tile), tile)
+        pick = jnp.where(doff_col[at][:, 0:1] == iota((tile, rows), 1), 1.0, 0.0).astype(BF16)
+        send_a[at] = (coef[at] * dot(pick, demb[...])).astype(BF16)
+
+    for c in range(chunks):
+
+        @pl.loop(0, n - 1)
+        def _(i):
+            rows_copy(send_a, recv_a, a_ssem, a_rsem, c, partner(i), me).start()
 
     own = pl.ds(pl.multiple_of(me * cap, cap), cap)
     recv_a[own] = send_a[own]
@@ -265,10 +286,23 @@
     scat_a[...] = jnp.zeros_like(scat_a)
     scat_d[...] = jnp.zeros_like(scat_d)
 
-    @pl.loop(0, n - 1)
-    def _(i):
-        p = partner(i)
-        rows_copy(send_a, recv_a, a_ssem, a_rsem, p, p).wait_recv()
+    for c in range(chunks):
+
+        @pl.loop(0, n - 1)
+        def _(i):
+            p = partner(i)
+            rows_copy(send_b, recv_b, b_ssem, b_rsem, c, p, p).wait_recv()
+
+    @pl.loop(0, tiles)
+    def _(k):
+        at = pl.ds(pl.multiple_of(k * tile, tile), tile)
+        grad = (coef[at] * recv_b[at].astype(F32)).astype(BF16)
+        put = jnp.where(iota((rows, tile), 0) == doff_row[k][0:1], 1.0, 0.0).astype(BF16)
+        scat_d[...] += dot(put, grad)
+
+    head_ref[...] = dot_t(scat_d[...].astype(BF16), donor_w[...])
+    head_out = pltpu.make_async_copy(head_ref, head_hbm, out_sem.at[1])
+    head_out.start()
 
     @pl.loop(0, tiles)
     def _(k):
@@ -276,29 +310,34 @@
         eye = iota((tile, tile), 0) == iota((tile, tile), 1)
         where = jnp.sum(jnp.where(eye, aoff_col[at][:, 0:1], 0), axis=0, keepdims=True)
         put = jnp.where(iota((rows, tile), 0) == where, 1.0, 0.0).astype(BF16)
-        scat_a[...] += dot(put, recv_a[at])
-
-    head_ref[...] = dot_t(scat_a[...].astype(BF16), acceptor_w[...])
-
-    @pl.loop(0, n - 1)
-    def _(i):
-        p = partner(i)
-        rows_copy(send_b, recv_b, b_ssem, b_rsem, p, p).wait_recv()
-
-    @pl.loop(0, tiles)
-    def _(k):
-        at = pl.ds(pl.multiple_of(k * tile, tile), tile)
-        grad = (coef[at] * recv_b[at].astype(F32)).astype(BF16)
-        put = jnp.where(iota((rows, tile), 0) == doff_row[k][0:1], 1.0, 0.0).astype(BF16)
-        scat_d[...] += dot(put, grad)
-
-    head_ref[...] += dot_t(scat_d[...].astype(BF16), donor_w[...])
-
-    @pl.loop(0, n - 1)
-    def _(i):
-        p = partner(i)
-        rows_copy(send_a, recv_a, a_ssem, a_rsem, p, me).wait_send()
-        rows_copy(send_b, recv_b, b_ssem, b_rsem, p, me).wait_send()
+        put_a[k] = put
+
+    block_out.wait()
+    head_out.wait()
+
+    for c in range(chunks):
+
+        @pl.loop(0, n - 1)
+        def _(i):
+            p = partner(i)
+            rows_copy(send_b, recv_b, b_ssem, b_rsem, c, p, me).wait_send()
+            rows_copy(send_a, recv_a, a_ssem, a_rsem, c, p, me).wait_send()
+            rows_copy(send_a, recv_a, a_ssem, a_rsem, c, p, p).wait_recv()
+
+    @pl.loop(0, tiles)
+    def _(k):
+        at = pl.ds(pl.multiple_of(k * tile, tile), tile)
+        scat_a[...] += dot(put_a[k], recv_a[at])
+
+    scat_out[...] = scat_a[...].astype(BF16)
+    last = pltpu.make_async_copy(scat_out, scat_hbm, out_sem.at[2])
+    last.start()
+    last.wait()
+
+
+def finish(block_ref, head_ref, scat_ref, proj_ref, block_out, head_out):
+    block_out[...] = block_ref[...]
+    head_out[...] = head_ref[...] + dot_t(scat_ref[...], proj_ref[...])
 
 
 def on_device(
@@ -326,14 +365,16 @@
     vmem = pl.BlockSpec(memory_space=pltpu.VMEM)
     hbm = pl.BlockSpec(memory_space=pl.ANY)
     dma = pltpu.SemaphoreType.DMA
-    return pl.pallas_call(
+    chunks = pair // WIDE
+    block, head, scat = pl.pallas_call(
         functools.partial(kernel, n, cap),
         out_shape=(
             jax.ShapeDtypeStruct((rows, channels), BF16),
             jax.ShapeDtypeStruct((rows, channels), F32),
+            jax.ShapeDtypeStruct((rows, pair), BF16),
         ),
         in_specs=[vmem, vmem, vmem, vmem, hbm, hbm, hbm, vmem, vmem, vmem, vmem, vmem],
-        out_specs=(vmem, vmem),
+        out_specs=(hbm, hbm, hbm),
         scratch_shapes=[
             pltpu.VMEM((rows + 2 * EDGE, channels), F32),
             pltpu.VMEM((rows, channels), F32),
@@ -342,7 +383,7 @@
             pltpu.VMEM((channels, pair), BF16),
             pltpu.VMEM((channels, pair), BF16),
             pltpu.VMEM((rows, pair), BF16),
-            pltpu.VMEM((rows, pair), BF16),
+            pltpu.VMEM((rows, WIDE), BF16),
             pltpu.VMEM((slots, pair), F32),
             pltpu.VMEM((slots, pair), BF16),
             pltpu.VMEM((slots, pair), BF16),
@@ -355,15 +396,21 @@
             pltpu.VMEM((slots, 128), I32),
             pltpu.VMEM((rows, pair), F32),
             pltpu.VMEM((rows, pair), F32),
+            pltpu.VMEM((slots, rows), BF16),
+            pltpu.VMEM((slots // tile, rows, tile), BF16),
+            pltpu.VMEM((rows, channels), BF16),
+            pltpu.VMEM((rows, channels), F32),
+            pltpu.VMEM((rows, pair), BF16),
             dma((taps + 2,)),
+            dma((3,)),
             dma((2,)),
             dma((2,)),
             dma((n,)),
             dma((n,)),
-            dma((n,)),
-            dma((n,)),
-            dma((n,)),
-            dma((n,)),
+            dma((chunks, n)),
+            dma((chunks, n)),
+            dma((chunks, n)),
+            dma((chunks, n)),
         ],
         compiler_params=pltpu.CompilerParams(
             collective_id=0, has_side_effects=True, vmem_limit_bytes=58 * 1024 * 1024
@@ -373,7 +420,7 @@
         features,
         bases.reshape(1, rows),
         base_table,
-        norm_gain.reshape(1, channels),
+        norm_gain,
         conv_weight,
         donor_proj,
         acceptor_proj,
@@ -383,6 +430,24 @@
         acceptor_offset.reshape(1, juncs),
         junction_cotangent,
     )
+    step = min(rows, 128)
+    line = pl.BlockSpec((step, channels), lambda i: (i, 0))
+    return pl.pallas_call(
+        finish,
+        grid=(rows // step,),
+        out_shape=(
+            jax.ShapeDtypeStruct((rows, channels), BF16),
+            jax.ShapeDtypeStruct((rows, channels), F32),
+        ),
+        in_specs=[
+            line,
+            line,
+            pl.BlockSpec((step, pair), lambda i: (i, 0)),
+            pl.BlockSpec((channels, pair), lambda i: (0, 0)),
+        ],
+        out_specs=(line, line),
+        name="finish",
+    )(block, head, scat, acceptor_proj)
 
 
 def solution(mesh):

time: 58.7 us -> 63.8 us (1.087)
  Pallas kernels: 53.2 us -> 62.9 us
  local copies, waits for them, and re-layouts: 4.59 us -> 0 us
    pallas_call x0 -> x1, Pallas kernels: none -> 5.44 us  [on_device(): pl.pallas_call(finish, grid=(rows // step,), out_shape=(jax.ShapeDtypeStr...]
    pallas_call x1, Pallas kernels: 53.2 us -> 57.5 us  [on_device(): pl.pallas_call(functools.partial(kernel, n, cap), out_shape=(jax.ShapeDty...]
    unnamed x4 -> x0, local copies, waits for them, and re-layouts: 3.33 us -> none
    reshape x1 -> x0, local copies, waits for them, and re-layouts: 1.26 us -> none  [on_device(): norm_gain.reshape(1, channels)]
where the time goes in v2:
time: 63.8 us; the launch traced here: 63.5 us
  Pallas kernels  62.9 us (99%)
  between operations  0.64 us (1%)
    pallas_call x1, Pallas kernels, on_device(): pl.pallas_call(functools.partial(kernel, n, cap), out_shape=(jax.ShapeDty...  57.5 us
    pallas_call x1, Pallas kernels, on_device(): pl.pallas_call(finish, grid=(rows // step,), out_shape=(jax.ShapeDtypeStr...  5.44 us

profile of v2, /device:TPU:0, one launch (start us, length us, event | category | flops | bytes accessed | tf_op | source)
XLA Modules:
  0.0 63.5 jit_solution(15466816287213398158)
XLA Ops:
  0.6 57.5 %block_and_pairs.1 = (bf16[512,768]{1,0:T(8,128)(2,1)}, f32[512,768]{1,0:T(8,128)}, bf16[512,768]{1,0:T(8,128)(2,1)}) custom-call(bf16[512,768]{1,0:T(8,128)(2,1)} %feat_ref.1, s32[1,512]{1,0:T(1,128)} %bitcast.4, bf16[4,768]{1,0:T(4,128)(2,1)} %table_ref.1, bf16[768]{0:T(1024)(128)(2,1)} %gain_ref.1, bf16[5,768,768]{2,1,0:T(8,128)(2,1)} %conv_hbm.1, ...), custom_call_target="tpu_custom_call" | custom-call | tf_op jit(solution)/shard_map/block_and_pairs/pallas_call | solution.py:369
  58.1 5.4 %finish.1 = (bf16[512,768]{1,0:T(8,128)(2,1)}, f32[512,768]{1,0:T(8,128)}) custom-call(bf16[512,768]{1,0:T(8,128)(2,1)} %get-tuple-element.5.block_ref, f32[512,768]{1,0:T(8,128)} %get-tuple-element.6.head_ref, bf16[512,768]{1,0:T(8,128)(2,1)} %get-tuple-element.7.scat_ref, bf16[768,768]{1,0:T(8,128)(2,1)} %proj_ref.1), custom_call_target="tpu_custom_call" | custom-call | tf_op jit(solution)/shard_map/finish/pallas_call | solution.py:435

commit v3 on v1

--- a/solution.py
+++ b/solution.py
@@ -68,6 +68,8 @@
     aoff_col,
     scat_a,
     scat_d,
+    put_a,
+    put_d,
     local_sem,
     halo_send,
     halo_recv,
@@ -100,8 +102,11 @@
         copy.start()
 
     def partner(i):
-        sign = 1 - 2 * lax.rem(i, 2)
-        return lax.rem(me + n // 2 + sign * ((i + 1) // 2), n)
+        half = i // 2
+        sign = 1 - 2 * lax.rem(half, 2)
+        near = lax.rem(i, 2)
+        step = (1 - near) * (n // 2) + sign * (1 - 2 * near) * ((half + 1) // 2 + near * (1 - lax.rem(half, 2)))
+        return lax.rem(me + n + step, n)
 
     barrier = pltpu.get_barrier_semaphore()
 
@@ -119,7 +124,7 @@
     embedded = feat_ref[...].astype(F32) + base
     emb[...] = embedded
     scale = lax.rsqrt(jnp.mean(embedded * embedded, axis=1, keepdims=True) + 1e-06)
-    normed = (embedded * scale * gain_ref[...].astype(F32)).astype(BF16)
+    normed = (embedded * scale * gain_ref[...].astype(F32)[None, :]).astype(BF16)
     npad[pl.ds(EDGE, rows)] = normed.astype(F32)
 
     owner_row = owner_ref[...]
@@ -262,8 +267,23 @@
     own = pl.ds(pl.multiple_of(me * cap, cap), cap)
     recv_a[own] = send_a[own]
     recv_b[own] = send_b[own]
-    scat_a[...] = jnp.zeros_like(scat_a)
-    scat_d[...] = jnp.zeros_like(scat_d)
+    if tiles > 1:
+        scat_a[...] = jnp.zeros_like(scat_a)
+        scat_d[...] = jnp.zeros_like(scat_d)
+
+    @pl.loop(0, tiles)
+    def _(k):
+        at = pl.ds(pl.multiple_of(k * tile, tile), tile)
+        eye = iota((tile, tile), 0) == iota((tile, tile), 1)
+        where = jnp.sum(jnp.where(eye, aoff_col[at][:, 0:1], 0), axis=0, keepdims=True)
+        put_a[k] = jnp.where(iota((rows, tile), 0) == where, 1.0, 0.0).astype(BF16)
+        put_d[k] = jnp.where(iota((rows, tile), 0) == doff_row[k][0:1], 1.0, 0.0).astype(BF16)
+
+    def scatter(total, put, values):
+        if tiles > 1:
+            total[...] += dot(put, values)
+        else:
+            total[...] = dot(put, values)
 
     @pl.loop(0, n - 1)
     def _(i):
@@ -273,10 +293,7 @@
     @pl.loop(0, tiles)
     def _(k):
         at = pl.ds(pl.multiple_of(k * tile, tile), tile)
-        eye = iota((tile, tile), 0) == iota((tile, tile), 1)
-        where = jnp.sum(jnp.where(eye, aoff_col[at][:, 0:1], 0), axis=0, keepdims=True)
-        put = jnp.where(iota((rows, tile), 0) == where, 1.0, 0.0).astype(BF16)
-        scat_a[...] += dot(put, recv_a[at])
+        scatter(scat_a, put_a[k], recv_a[at])
 
     head_ref[...] = dot_t(scat_a[...].astype(BF16), acceptor_w[...])
 
@@ -289,8 +306,7 @@
     def _(k):
         at = pl.ds(pl.multiple_of(k * tile, tile), tile)
         grad = (coef[at] * recv_b[at].astype(F32)).astype(BF16)
-        put = jnp.where(iota((rows, tile), 0) == doff_row[k][0:1], 1.0, 0.0).astype(BF16)
-        scat_d[...] += dot(put, grad)
+        scatter(scat_d, put_d[k], grad)
 
     head_ref[...] += dot_t(scat_d[...].astype(BF16), donor_w[...])
 
@@ -355,6 +371,8 @@
             pltpu.VMEM((slots, 128), I32),
             pltpu.VMEM((rows, pair), F32),
             pltpu.VMEM((rows, pair), F32),
+            pltpu.VMEM((slots // tile, rows, tile), BF16),
+            pltpu.VMEM((slots // tile, rows, tile), BF16),
             dma((taps + 2,)),
             dma((2,)),
             dma((2,)),
@@ -373,7 +391,7 @@
         features,
         bases.reshape(1, rows),
         base_table,
-        norm_gain.reshape(1, channels),
+        norm_gain,
         conv_weight,
         donor_proj,
         acceptor_proj,

time: 58.7 us -> 57.4 us (0.978)
  local copies, waits for them, and re-layouts: 4.59 us -> 3.33 us
    reshape x1 -> x0, local copies, waits for them, and re-layouts: 1.26 us -> none  [on_device(): norm_gain.reshape(1, channels)]
where the time goes in v3:
time: 57.4 us; the launch traced here: 57.3 us
  Pallas kernels  53.3 us (93%)
  local copies, waits for them, and re-layouts  3.33 us (6%)
  between operations  0.65 us (1%)
    pallas_call x1, Pallas kernels, on_device(): pl.pallas_call(functools.partial(kernel, n, cap), out_shape=(jax.ShapeDty...  53.3 us
    unnamed x4, local copies, waits for them, and re-layouts  3.33 us

profile of v3, /device:TPU:0, one launch (start us, length us, event | category | flops | bytes accessed | tf_op | source)
XLA Modules:
  0.0 57.3 jit_solution(1437764025493969822)
XLA Ops:
  0.6 53.3 %block_and_pairs.1 = (bf16[512,768]{1,0:T(8,128)(2,1)}, f32[512,768]{1,0:T(8,128)}) custom-call(bf16[512,768]{1,0:T(8,128)(2,1)} %feat_ref.1, s32[1,512]{1,0:T(1,128)} %bitcast.4, bf16[4,768]{1,0:T(4,128)(2,1)} %table_ref.1, bf16[768]{0:T(1024)(128)(2,1)} %gain_ref.1, bf16[5,768,768]{2,1,0:T(8,128)(2,1)} %conv_hbm.1, bf16[768,768]{1,0:T(8,128)(2,1)} %donor_hbm.1, ...), custom_call_target="tpu_custom_call" | custom-call | tf_op jit(solution)/shard_map/block_and_pairs/pallas_call | solution.py:345
  53.9 0.0 copy-start
  53.9 2.2 %copy.16 = bf16[512,768]{1,0:T(8,128)(2,1)} copy(bf16[512,768]{1,0:T(8,128)(2,1)} %get-tuple-element.4) | data formatting | bytes 1572864
  56.1 0.0 copy-done
  56.1 1.1 %copy.17 = f32[512,768]{1,0:T(8,128)} copy(f32[512,768]{1,0:T(8,128)S(1)} %copy-done) | data formatting | bytes 3145728
Async XLA Ops:
  53.9 2.2 %copy-start = (f32[512,768]{1,0:T(8,128)S(1)}, f32[512,768]{1,0:T(8,128)}, u32[]{:S(2)}) copy-start(f32[512,768]{1,0:T(8,128)} %get-tuple-element.5) | copy-start | bytes 4718596
